TPU v7x, 256 devices: a whole 4x4x8 slice. The times are simulated.
256 devices in a mesh: seq: 16 (over x, y), head: 16 (over z, core).
Axes of the slice: x: 4, y: 4, z: 8, core: 2. Of those that a mesh axis runs over, the one named last changes fastest.
Arguments:
- queries: bfloat16 [16384, 4096], P('seq', 'head'), may hold values from -100 to 100
- states: bfloat16 [4096, 8192], P('seq', 'head'), may hold values from -6 to 6
- key_weight: bfloat16 [8192, 4096], P(None, 'head'), may hold values from -0.0625 to 0.0625
- value_weight: bfloat16 [8192, 4096], P(None, 'head'), may hold values from -0.0625 to 0.0625
- neighbour_ids: int32 [256, 2], P('seq'), may hold values from 0 to 31, all different within a row
- out_grad: bfloat16 [16384, 4096], P('seq', 'head'), may hold values from -4 to 4
Outputs:
- context: bfloat16 [16384, 4096], P('seq', 'head')
- query_grad: bfloat16 [16384, 4096], P('seq', 'head')
- key_weight_grad: float32 [8192, 4096], P('seq', 'head')
- value_weight_grad: float32 [8192, 4096], P('seq', 'head')
Inputs may be any that keep to these rules, and one draw needn't show every extreme that they name: `neighbour_ids`: each span names 2 different pool blocks, and every block is named by some span.
All inputs are finite; a program needn't handle non-finite values.
Results may differ from a plain program's by a relative error of at most 0.04.
Values may be sent and summed in bfloat16 or wider, within the bound.
A program may use at most 128 MiB of HBM per device.

v0:
```python
import math
import jax
import jax.numpy as jnp
from jax import lax
from jax.sharding import PartitionSpec as P

HD = 128
SPAN = 64
NBR = 128
TOPN = 2


def local(queries, states, key_weight, value_weight, neighbour_ids, out_grad):
    head_cols = queries.shape[1]
    heads_here = head_cols // HD
    own_rows = states.shape[0]
    seq_count = lax.axis_size("seq")
    pool_total = own_rows * seq_count
    block_count = pool_total // NBR
    span_count = neighbour_ids.shape[0]
    score_scale = 1.0 / math.sqrt(HD)
    full_states = lax.all_gather(states, "head", axis=1, tiled=True)
    own_keys = jnp.dot(full_states, key_weight, preferred_element_type=jnp.float32).astype(
        jnp.bfloat16
    )
    own_values = jnp.dot(full_states, value_weight, preferred_element_type=jnp.float32).astype(
        jnp.bfloat16
    )
    pool_keys, pool_values = (
        lax.all_gather(own_keys, "seq", axis=0, tiled=True),
        lax.all_gather(own_values, "seq", axis=0, tiled=True),
    )
    key_rows = pool_keys.reshape(block_count, NBR, head_cols)[neighbour_ids]
    key_rows = key_rows.reshape(span_count, TOPN * NBR, heads_here, HD)
    value_rows = pool_values.reshape(block_count, NBR, head_cols)[neighbour_ids]
    value_rows = value_rows.reshape(span_count, TOPN * NBR, heads_here, HD)
    queries_here = queries.reshape(span_count, SPAN, heads_here, HD)
    grad_here = out_grad.reshape(span_count, SPAN, heads_here, HD)
    scores = (
        jnp.einsum("cqhd,ckhd->chqk", queries_here, key_rows, preferred_element_type=jnp.float32)
        * score_scale
    )
    soft_weights = jax.nn.softmax(scores, axis=-1)
    weights_low = soft_weights.astype(jnp.bfloat16)
    context = jnp.einsum(
        "chqk,ckhd->cqhd", weights_low, value_rows, preferred_element_type=jnp.float32
    ).astype(jnp.bfloat16)
    prob_grad = jnp.einsum(
        "cqhd,ckhd->chqk", grad_here, value_rows, preferred_element_type=jnp.float32
    )
    row_delta = jnp.sum(soft_weights * prob_grad, axis=-1, keepdims=True)
    score_grad = (soft_weights * (prob_grad - row_delta) * score_scale).astype(jnp.bfloat16)
    query_grad = jnp.einsum(
        "chqk,ckhd->cqhd", score_grad, key_rows, preferred_element_type=jnp.float32
    ).astype(jnp.bfloat16)
    key_part = jnp.einsum(
        "chqk,cqhd->ckhd", score_grad, queries_here, preferred_element_type=jnp.float32
    )
    value_part = jnp.einsum(
        "chqk,cqhd->ckhd", weights_low, grad_here, preferred_element_type=jnp.float32
    )
    both_parts = jnp.concatenate(
        [
            key_part.reshape(span_count * TOPN, NBR, head_cols),
            value_part.reshape(span_count * TOPN, NBR, head_cols),
        ],
        axis=2,
    )
    parts_high = both_parts.astype(jnp.bfloat16)
    parts_rest = (both_parts - parts_high.astype(jnp.float32)).astype(jnp.bfloat16)
    flat_ids = neighbour_ids.reshape(-1)
    block_range = jnp.arange(own_rows * lax.axis_size("seq") // NBR, dtype=jnp.int32)
    block_picks = (flat_ids[:, None] == block_range[None, :]).astype(jnp.bfloat16)
    summed_rows = jnp.einsum(
        "jb,jrc->brc", block_picks, parts_high, preferred_element_type=jnp.float32
    )
    summed_rows = summed_rows + jnp.einsum(
        "jb,jrc->brc", block_picks, parts_rest, preferred_element_type=jnp.float32
    )
    own_grad = lax.psum_scatter(
        summed_rows.reshape(own_rows * lax.axis_size("seq"), 2 * head_cols).astype(jnp.bfloat16),
        "seq",
        scatter_dimension=0,
        tiled=True,
    )
    weight_grads_all = lax.psum_scatter(
        jnp.einsum("rf,rc->fc", full_states, own_grad, preferred_element_type=jnp.float32).astype(
            jnp.bfloat16
        ),
        "seq",
        scatter_dimension=0,
        tiled=True,
    ).astype(jnp.float32)
    return (
        context.reshape(span_count * SPAN, head_cols),
        query_grad.reshape(span_count * SPAN, head_cols),
        weight_grads_all[:, :head_cols],
        weight_grads_all[:, head_cols:],
    )


def solution(mesh):
    in_specs = (
        P("seq", "head"),
        P("seq", "head"),
        P(None, "head"),
        P(None, "head"),
        P("seq", None),
        P("seq", "head"),
    )
    out_specs = (P("seq", "head"), P("seq", "head"), P("seq", "head"), P("seq", "head"))
    return jax.shard_map(local, mesh=mesh, in_specs=in_specs, out_specs=out_specs, check_vma=False)
```

profile of v0, /device:TPU:2, one launch (start us, length us, event | category | flops | bytes accessed | tf_op | source)
XLA Modules:
  0.0 437.8 jit_solution(14851394914533141190)
XLA Ops:
  7.9 47.0 %all-gather.4.cloned.1.call-done = bf16[256,8192]{1,0:T(8,128)(2,1)} async-done(((bf16[256,512]{1,0:T(8,128)(2,1)}), bf16[256,8192]{1,0:T(8,128)(2,1)}) %all-gather.4.cloned.1.call-update) | async-done | bytes 4194320 | tf_op jit(solution)/shard_map/all_gather | solution.py:22
  55.0 5.4 %convolution_convert_fusion.1 = bf16[256,256]{1,0:T(8,128)(2,1)} fusion(bf16[256,8192]{1,0:T(8,128)(2,1)} %all-gather.4.cloned.1.call-done, bf16[8192,256]{1,0:T(8,128)(2,1)} %param.8), kind=kOutput, calls=%fused_computation.36 | convolution fusion | flops 1073807360 | bytes 8519680 | tf_op jit(solution)/shard_map/dot_general | solution.py:23
  60.4 5.4 %convolution_convert_fusion.2 = bf16[256,256]{1,0:T(8,128)(2,1)} fusion(bf16[256,8192]{1,0:T(8,128)(2,1)} %all-gather.4.cloned.1.call-done, bf16[8192,256]{1,0:T(8,128)(2,1)} %param.9), kind=kOutput, calls=%fused_computation.37 | convolution fusion | flops 1073807360 | bytes 8519680 | tf_op jit(solution)/shard_map/dot_general | solution.py:26
  66.8 41.9 %all-gather.8.cloned.1.call-done = bf16[4096,256]{1,0:T(8,128)(2,1)} async-done(((bf16[256,256]{1,0:T(8,128)(2,1)}), bf16[4096,256]{1,0:T(8,128)(2,1)}) %all-gather.8.cloned.1.call-update) | async-done | bytes 2097168 | tf_op jit(solution)/shard_map/all_gather | solution.py:30
  108.7 3.6 gather_fusion.1
  114.9 46.3 %all-gather.6.cloned.1.call-done = bf16[4096,256]{1,0:T(8,128)(2,1)} async-done(((bf16[256,256]{1,0:T(8,128)(2,1)}), bf16[4096,256]{1,0:T(8,128)(2,1)}) %all-gather.6.cloned.1.call-update) | async-done | bytes 2097168 | tf_op jit(solution)/shard_map/all_gather | solution.py:31
  161.1 3.6 gather_fusion
  164.7 4.0 reshape.77
  174.8 8.5 %convolution_bitcast_fusion = f32[16,256,2,128]{3,1,2,0:T(8,128)} fusion(bf16[16,64,2,128]{3,2,1,0:T(2,128)(2,1)S(1)} %reshape.50, f32[16,2,64]{2,1,0:T(2,128)S(1)} %get-tuple-element.18, f32[16,2,256,64]{2,3,1,0:T(8,128)} %copy-done.3), kind=kOutput, calls=%fused_computation.12 | convolution fusion | flops 136841472 | bytes 6823936 | tf_op jit(solution)/shard_map/chqk,cqhd->ckhd/dot_general | solution.py:59
  183.3 17.6 %convolution_bitcast_fusion.1 = f32[16,256,2,128]{3,1,2,0:T(8,128)} fusion(f32[16,2,256,64]{2,3,1,0:T(8,128)} %fusion.19, bf16[16,64,2,128]{3,2,1,0:T(2,128)(2,1)S(1)} %reshape.48, f32[16,2,64,256]{3,2,1,0:T(8,128)} %get-tuple-element.19, f32[16,2,64]{2,1,0:T(2,128)S(1)} %get-tuple-element.18), kind=kOutput, calls=%fused_computation.13 | convolution fusion | flops 137890048 | bytes 8921088 | tf_op jit(solution)/shard_map/chqk,cqhd->ckhd/dot_general | solution.py:56
  200.9 5.5 %copy.50 = f32[16,256,2,128]{1,0,3,2:T(8,128)} copy(f32[16,256,2,128]{3,1,2,0:T(8,128)} %convolution_bitcast_fusion.1) | data formatting | bytes 8388608 | tf_op jit(solution)/shard_map/chqk,cqhd->ckhd/transpose | solution.py:56
  206.4 4.7 %reshape.52 = f32[32,128,256]{1,0,2:T(8,128)} reshape(f32[16,256,2,128]{1,0,3,2:T(8,128)} %copy.50) | data formatting | bytes 8388608 | tf_op jit(solution)/shard_map/reshape | solution.py:64
  211.1 5.6 %copy.53 = f32[32,128,256]{2,0,1:T(8,128)} copy(f32[32,128,256]{1,0,2:T(8,128)} %reshape.52) | data formatting | bytes 8388608 | tf_op jit(solution)/shard_map/reshape | solution.py:64
  216.7 5.5 %copy.52 = f32[16,256,2,128]{1,0,3,2:T(8,128)} copy(f32[16,256,2,128]{3,1,2,0:T(8,128)} %convolution_bitcast_fusion) | data formatting | bytes 8388608 | tf_op jit(solution)/shard_map/chqk,cqhd->ckhd/transpose | solution.py:59
  222.2 4.7 %reshape.53 = f32[32,128,256]{1,0,2:T(8,128)} reshape(f32[16,256,2,128]{1,0,3,2:T(8,128)} %copy.52) | data formatting | bytes 8388608 | tf_op jit(solution)/shard_map/reshape | solution.py:65
  226.9 5.6 %copy.54 = f32[32,128,256]{2,0,1:T(8,128)} copy(f32[32,128,256]{1,0,2:T(8,128)} %reshape.53) | data formatting | bytes 8388608 | tf_op jit(solution)/shard_map/reshape | solution.py:65
  232.5 4.8 %fusion.4 = f32[32,128,512]{2,0,1:T(8,128)S(1)} fusion(f32[32,128,256]{2,0,1:T(8,128)} %copy.54, f32[32,128,256]{2,0,1:T(8,128)} %copy.53, s32[32]{0:T(128)S(1)} %eq.15), kind=kOutput, calls=%fused_computation.10 | convolution fusion | flops 142607360 | bytes 16777344 | tf_op jit(solution)/shard_map/jb,jrc->brc/dot_general | solution.py:74
  238.5 2.8 add_convert_fusion
  241.3 6.5 %copy.55 = bf16[32,128,512]{2,1,0:T(8,128)(2,1)} copy(bf16[32,128,512]{2,0,1:T(8,128)(2,1)} %add_convert_fusion) | data formatting | bytes 8388608 | tf_op jit(solution)/shard_map/convert_element_type | solution.py:81
  247.8 82.2 %reduce-scatter.3.cloned.1.call-done = bf16[256,512]{1,0:T(8,128)(2,1)} async-done(((bf16[4096,512]{1,0:T(8,128)(2,1)}), bf16[256,512]{1,0:T(8,128)(2,1)}) %reduce-scatter.3.cloned.1.call-update) | async-done | bytes 262160 | tf_op jit(solution)/shard_map/reduce_scatter | solution.py:80
  330.0 7.9 %fusion.2 = bf16[8192,512]{0,1:T(8,128)(2,1)} fusion(bf16[256,512]{1,0:T(8,128)(2,1)} %reduce-scatter.3.cloned.1.call-done, bf16[256,8192]{1,0:T(8,128)(2,1)} %all-gather.4.cloned.1.call-done), kind=kOutput, calls=%fused_computation.5 | convolution fusion | flops 2151677952 | bytes 12845056 | tf_op jit(solution)/shard_map/rf,rc->fc/dot_general | solution.py:87
  337.9 14.7 %fusion.29 = bf16[16,64,2,128]{3,1,2,0:T(8,128)(2,1)S(1)} fusion(bf16[16,256,2,128]{3,2,1,0:T(2,128)(2,1)S(1)} %reshape.78, f32[16,2,256,64]{2,3,1,0:T(8,128)} %fusion.19, f32[16,2,64,256]{3,2,1,0:T(8,128)} %get-tuple-element.19, f32[16,2,64]{2,1,0:T(2,128)S(1)} %get-tuple-element.18), kind=kOutput, calls=%fused_computation.34 | convolution fusion | flops 138152192 | bytes 6823936 | tf_op jit(solution)/shard_map/chqk,ckhd->cqhd/dot_general | solution.py:53
  353.2 6.6 %fusion.32 = bf16[16,64,2,128]{3,1,2,0:T(8,128)(2,1)S(1)} fusion(bf16[16,256,2,128]{3,2,1,0:T(2,128)(2,1)} %reshape.77, f32[16,2,64]{2,1,0:T(2,128)S(1)} %get-tuple-element.18, f32[16,2,256,64]{2,3,1,0:T(8,128)} %copy-done.3), kind=kOutput, calls=%fused_computation.35 | convolution fusion | flops 137103616 | bytes 4726784 | tf_op jit(solution)/shard_map/chqk,ckhd->cqhd/dot_general | solution.py:45
  361.4 66.7 %reduce-scatter.5.cloned.1.call-done = bf16[512,512]{0,1:T(8,128)(2,1)} async-done(((bf16[8192,512]{0,1:T(8,128)(2,1)}), bf16[512,512]{0,1:T(8,128)(2,1)}) %reduce-scatter.5.cloned.1.call-update) | async-done | bytes 524304 | tf_op jit(solution)/shard_map/reduce_scatter | solution.py:86
  (42 shorter events, 16.8 us)
Async XLA Ops:
  7.2 47.8 %all-gather.4.cloned.1.call-start = ((), (), s32[]{:S(2)}) async-start(), calls=%async_computation.2 | async-start | bytes 4456448 | tf_op jit(solution)/shard_map/all_gather | solution.py:22
  7.9 100.8 %all-gather.8.cloned.1.call-start = ((), (), s32[]{:S(2)}) async-start(), calls=%async_computation.4 | async-start | bytes 2228224 | tf_op jit(solution)/shard_map/all_gather | solution.py:30
  60.4 5.8 %copy-start.6 = (s32[16,2]{0,1:T(2,128)S(1)}, s32[16,2]{0,1:T(2,128)}, u32[]{:S(2)}) copy-start(s32[16,2]{0,1:T(2,128)} %param.10) | copy-start | bytes 388
  60.4 6.1 %copy-start.4 = (bf16[1024,256]{1,0:T(8,128)(2,1)S(1)}, bf16[1024,256]{1,0:T(8,128)(2,1)}, u32[]{:S(2)}) copy-start(bf16[1024,256]{1,0:T(8,128)(2,1)} %param.6) | copy-start | bytes 1572868
  60.4 6.3 %copy-start.5 = (bf16[1024,256]{1,0:T(8,128)(2,1)S(1)}, bf16[1024,256]{1,0:T(8,128)(2,1)}, u32[]{:S(2)}) copy-start(bf16[1024,256]{1,0:T(8,128)(2,1)} %param.11) | copy-start | bytes 1572868
  60.4 100.7 %all-gather.6.cloned.1.call-start = ((), (), s32[]{:S(2)}) async-start(), calls=%async_computation.3 | async-start | bytes 2228224 | tf_op jit(solution)/shard_map/all_gather | solution.py:31
  65.9 264.1 %reduce-scatter.3.cloned.1.call-start = ((), (), s32[]{:S(2)}) async-start(), calls=%async_computation.5 | async-start | bytes 4456448 | tf_op jit(solution)/shard_map/reduce_scatter | solution.py:80
  169.5 2.1 copy-start.3
  169.5 3.1 copy-start.2
  232.5 4.8 %copy-start = (f32[32,128,256]{2,0,1:T(8,128)S(1)}, f32[32,128,256]{2,0,1:T(8,128)}, u32[]{:S(2)}) copy-start(f32[32,128,256]{2,0,1:T(8,128)} %copy.53) | copy-start | bytes 12582916
  232.5 5.9 %copy-start.1 = (f32[32,128,256]{2,0,1:T(8,128)S(1)}, f32[32,128,256]{2,0,1:T(8,128)}, u32[]{:S(2)}) copy-start(f32[32,128,256]{2,0,1:T(8,128)} %copy.54) | copy-start | bytes 12582916
  247.8 180.4 %reduce-scatter.5.cloned.1.call-start = ((), (), s32[]{:S(2)}) async-start(), calls=%async_computation.6 | async-start | bytes 8912896 | tf_op jit(solution)/shard_map/reduce_scatter | solution.py:86
Sparse Core Ops, SparseCore 0:
  9.8 45.0 all-gather.3
  60.5 48.1 all-gather.7
  111.7 49.3 all-gather.5
  247.9 82.0 reduce-scatter.2
  338.0 90.0 reduce-scatter.4
where the time goes:
time: 439 us; the launch traced here: 438 us
  waiting for transfers between devices  285 us (65%)
  matrix products  76.7 us (17%)
  local copies, waits for them, and re-layouts  60.1 us (14%)
  between operations  13.9 us (3%)
    reduce_scatter x1, waiting for transfers between devices, local(): lax.psum_scatter(summed_rows.reshape(own_rows * lax.axis_size('seq'), 2 *...  82.2 us
    reduce_scatter x1, waiting for transfers between devices, local(): lax.psum_scatter(jnp.einsum('rf,rc->fc', full_states, own_grad, preferred...  66.7 us
    all_gather x1, waiting for transfers between devices, local(): full_states = lax.all_gather(states, 'head', axis=1, tiled=True)  47 us
    all_gather x1, waiting for transfers between devices, local(): lax.all_gather(own_values, 'seq', axis=0, tiled=True)  46.3 us
    all_gather x1, waiting for transfers between devices, local(): lax.all_gather(own_keys, 'seq', axis=0, tiled=True)  41.9 us
    dot_general x1, matrix products, local(): jnp.einsum('chqk,cqhd->ckhd', score_grad, queries_here, preferred_element...  17.6 us
    dot_general x1, matrix products, local(): jnp.einsum('chqk,ckhd->cqhd', score_grad, key_rows, preferred_element_typ...  14.7 us
    reshape x2, local copies, waits for them, and re-layouts, local(): key_part.reshape(span_count * TOPN, NBR, head_cols)  10.3 us
  transfers between devices with their start and end apart: 5, of which 5 were waited for; matrix products, arithmetic and copies ran while one was open for 8% of the time, Pallas kernels for 0%

commit v1 on v0

--- a/solution.py
+++ b/solution.py
@@ -10,6 +10,11 @@
 TOPN = 2
 
 
+def gather_from_all(array, axis, dim):
+    copies = jnp.concatenate([array] * lax.axis_size(axis), axis=dim)
+    return lax.all_to_all(copies, axis, dim, dim, tiled=True)
+
+
 def local(queries, states, key_weight, value_weight, neighbour_ids, out_grad):
     head_cols = queries.shape[1]
     heads_here = head_cols // HD
@@ -19,7 +24,7 @@
     block_count = pool_total // NBR
     span_count = neighbour_ids.shape[0]
     score_scale = 1.0 / math.sqrt(HD)
-    full_states = lax.all_gather(states, "head", axis=1, tiled=True)
+    full_states = gather_from_all(states, "head", 1)
     own_keys = jnp.dot(full_states, key_weight, preferred_element_type=jnp.float32).astype(
         jnp.bfloat16
     )

time: 439 us -> 508 us (1.16)
  blocking collectives: 0 us -> 103 us
  waiting for transfers between devices: 285 us -> 236 us
  local copies, waits for them, and re-layouts: 60.1 us -> 74 us
    all_to_all x0 -> x1, blocking collectives: none -> 103 us  [gather_from_all(): return lax.all_to_all(copies, axis, dim, dim, tiled=True)]
    all_gather x1 -> x0, waiting for transfers between devices: 47 us -> none  [local(): full_states = lax.all_gather(states, 'head', axis=1, tiled=True)]
    all_to_all x0 -> x2, local copies, waits for them, and re-layouts: none -> 12.8 us  [gather_from_all(): return lax.all_to_all(copies, axis, dim, dim, tiled=True)]
  transfers between devices with their start and end apart: 5 -> 4, of which waited for: 5 -> 4; matrix products, arithmetic and copies ran while one was open for 8% -> 7% of each run, Pallas kernels for 0% -> 0%
where the time goes in v1:
time: 508 us; the launch traced here: 507 us
  waiting for transfers between devices  236 us (46%)
  blocking collectives  103 us (20%)
  matrix products  76.7 us (15%)
  local copies, waits for them, and re-layouts  74 us (15%)
  between operations  14.1 us (3%)
    all_to_all x1, blocking collectives, gather_from_all(): return lax.all_to_all(copies, axis, dim, dim, tiled=True)  103 us
    reduce_scatter x1, waiting for transfers between devices, local(): lax.psum_scatter(summed_rows.reshape(own_rows * lax.axis_size('seq'), 2 *...  82.2 us
    reduce_scatter x1, waiting for transfers between devices, local(): lax.psum_scatter(jnp.einsum('rf,rc->fc', full_states, own_grad, preferred...  66.1 us
    all_gather x1, waiting for transfers between devices, local(): lax.all_gather(own_values, 'seq', axis=0, tiled=True)  46.2 us
    all_gather x1, waiting for transfers between devices, local(): lax.all_gather(own_keys, 'seq', axis=0, tiled=True)  41.9 us
    dot_general x1, matrix products, local(): jnp.einsum('chqk,cqhd->ckhd', score_grad, queries_here, preferred_element...  17.6 us
    dot_general x1, matrix products, local(): jnp.einsum('chqk,ckhd->cqhd', score_grad, key_rows, preferred_element_typ...  14.7 us
    all_to_all x2, local copies, waits for them, and re-layouts, gather_from_all(): return lax.all_to_all(copies, axis, dim, dim, tiled=True)  12.8 us
  transfers between devices with their start and end apart: 4, of which 4 were waited for; matrix products, arithmetic and copies ran while one was open for 7% of the time, Pallas kernels for 0%

profile of v1, /device:TPU:2, one launch (start us, length us, event | category | flops | bytes accessed | tf_op | source)
XLA Modules:
  0.0 506.8 jit_solution(8786744350833485609)
XLA Ops:
  10.7 6.4 %copy.87 = bf16[256,16,512]{2,0,1:T(8,128)(2,1)} copy(bf16[256,16,512]{0,2,1:T(8,128)(2,1)} %bitcast.89) | data formatting | bytes 8388608 | tf_op jit(solution)/shard_map/all_to_all | solution.py:15
  17.1 103.3 %all_to_all.12 = bf16[256,16,512]{2,0,1:T(8,128)(2,1)} all-to-all(bf16[256,16,512]{2,0,1:T(8,128)(2,1)} %copy.87), channel_id=1, replica_groups=mesh['seq'=16,'head'=16] {'head'}, dimensions={1} | all-to-all | bytes 8388608 | tf_op jit(solution)/shard_map/all_to_all | solution.py:15
  120.5 6.4 %copy.88 = bf16[256,16,512]{0,2,1:T(8,128)(2,1)} copy(bf16[256,16,512]{2,0,1:T(8,128)(2,1)} %all_to_all.12) | data formatting | bytes 8388608 | tf_op jit(solution)/shard_map/all_to_all | solution.py:15
  126.8 5.4 %convolution_convert_fusion.1 = bf16[256,256]{1,0:T(8,128)(2,1)} fusion(bf16[256,8192]{0,1:T(8,128)(2,1)} %bitcast.85, bf16[8192,256]{1,0:T(8,128)(2,1)} %param.8), kind=kOutput, calls=%fused_computation.35 | convolution fusion | flops 1073807360 | bytes 8519680 | tf_op jit(solution)/shard_map/dot_general | solution.py:28
  132.4 5.5 %convolution_convert_fusion.2 = bf16[256,256]{1,0:T(8,128)(2,1)} fusion(bf16[256,8192]{0,1:T(8,128)(2,1)} %bitcast.86, bf16[8192,256]{1,0:T(8,128)(2,1)} %param.9), kind=kOutput, calls=%fused_computation.36 | convolution fusion | flops 1073807360 | bytes 8519680 | tf_op jit(solution)/shard_map/dot_general | solution.py:31
  138.8 41.9 %all-gather.5.cloned.1.call-done = bf16[4096,256]{1,0:T(8,128)(2,1)} async-done(((bf16[256,256]{1,0:T(8,128)(2,1)}), bf16[4096,256]{1,0:T(8,128)(2,1)}) %all-gather.5.cloned.1.call-update) | async-done | bytes 2097168 | tf_op jit(solution)/shard_map/all_gather | solution.py:35
  186.8 46.2 %all-gather.3.cloned.1.call-done = bf16[4096,256]{1,0:T(8,128)(2,1)} async-done(((bf16[256,256]{1,0:T(8,128)(2,1)}), bf16[4096,256]{1,0:T(8,128)(2,1)}) %all-gather.3.cloned.1.call-update) | async-done | bytes 2097168 | tf_op jit(solution)/shard_map/all_gather | solution.py:36
  233.0 3.6 gather_fusion
  236.7 4.0 reshape.79
  245.6 8.5 %convolution_bitcast_fusion = f32[16,256,2,128]{3,1,2,0:T(8,128)} fusion(bf16[16,64,2,128]{3,2,1,0:T(2,128)(2,1)S(1)} %reshape.52, f32[16,2,64]{2,1,0:T(2,128)S(1)} %get-tuple-element.6, f32[16,2,256,64]{2,3,1,0:T(8,128)} %copy-done.3), kind=kOutput, calls=%fused_computation.11 | convolution fusion | flops 136841472 | bytes 6823936 | tf_op jit(solution)/shard_map/chqk,cqhd->ckhd/dot_general | solution.py:64
  254.1 17.6 %convolution_bitcast_fusion.1 = f32[16,256,2,128]{3,1,2,0:T(8,128)} fusion(f32[16,2,256,64]{2,3,1,0:T(8,128)} %fusion.18, bf16[16,64,2,128]{3,2,1,0:T(2,128)(2,1)S(1)} %reshape.50, f32[16,2,64,256]{3,2,1,0:T(8,128)} %get-tuple-element.7, f32[16,2,64]{2,1,0:T(2,128)S(1)} %get-tuple-element.6), kind=kOutput, calls=%fused_computation.12 | convolution fusion | flops 137890048 | bytes 8921088 | tf_op jit(solution)/shard_map/chqk,cqhd->ckhd/dot_general | solution.py:61
  271.7 5.5 %copy.102 = f32[16,256,2,128]{1,0,3,2:T(8,128)} copy(f32[16,256,2,128]{3,1,2,0:T(8,128)} %convolution_bitcast_fusion.1) | data formatting | bytes 8388608 | tf_op jit(solution)/shard_map/chqk,cqhd->ckhd/transpose | solution.py:61
  277.2 4.7 reshape.54
  282.0 5.6 %copy.105 = f32[32,128,256]{2,0,1:T(8,128)} copy(f32[32,128,256]{1,0,2:T(8,128)} %reshape.54) | data formatting | bytes 8388608 | tf_op jit(solution)/shard_map/reshape | solution.py:69
  287.6 5.5 %copy.104 = f32[16,256,2,128]{1,0,3,2:T(8,128)} copy(f32[16,256,2,128]{3,1,2,0:T(8,128)} %convolution_bitcast_fusion) | data formatting | bytes 8388608 | tf_op jit(solution)/shard_map/chqk,cqhd->ckhd/transpose | solution.py:64
  293.1 4.7 reshape.55
  297.8 5.6 %copy.106 = f32[32,128,256]{2,0,1:T(8,128)} copy(f32[32,128,256]{1,0,2:T(8,128)} %reshape.55) | data formatting | bytes 8388608 | tf_op jit(solution)/shard_map/reshape | solution.py:70
  303.4 4.8 fusion.3
  312.1 6.5 %copy.107 = bf16[32,128,512]{2,1,0:T(8,128)(2,1)} copy(bf16[32,128,512]{2,0,1:T(8,128)(2,1)} %add_convert_fusion) | data formatting | bytes 8388608 | tf_op jit(solution)/shard_map/convert_element_type | solution.py:86
  318.6 82.2 %reduce-scatter.3.cloned.1.call-done = bf16[256,512]{1,0:T(8,128)(2,1)} async-done(((bf16[4096,512]{1,0:T(8,128)(2,1)}), bf16[256,512]{1,0:T(8,128)(2,1)}) %reduce-scatter.3.cloned.1.call-update) | async-done | bytes 262160 | tf_op jit(solution)/shard_map/reduce_scatter | solution.py:85
  400.8 7.8 %convolution_convert_fusion = bf16[8192,512]{1,0:T(8,128)(2,1)} fusion(bf16[256,8192]{0,1:T(8,128)(2,1)} %bitcast.87, bf16[256,512]{1,0:T(8,128)(2,1)} %reduce-scatter.3.cloned.1.call-done), kind=kOutput, calls=%fused_computation.4 | convolution fusion | flops 2151677952 | bytes 12845056 | tf_op jit(solution)/shard_map/rf,rc->fc/dot_general | solution.py:92
  408.6 14.7 %fusion.28 = bf16[16,64,2,128]{3,1,2,0:T(8,128)(2,1)S(1)} fusion(bf16[16,256,2,128]{3,2,1,0:T(2,128)(2,1)S(1)} %reshape.80, f32[16,2,256,64]{2,3,1,0:T(8,128)} %fusion.18, f32[16,2,64,256]{3,2,1,0:T(8,128)} %get-tuple-element.7, f32[16,2,64]{2,1,0:T(2,128)S(1)} %get-tuple-element.6), kind=kOutput, calls=%fused_computation.33 | convolution fusion | flops 138152192 | bytes 6823936 | tf_op jit(solution)/shard_map/chqk,ckhd->cqhd/dot_general | solution.py:58
  423.9 6.6 %fusion.31 = bf16[16,64,2,128]{3,1,2,0:T(8,128)(2,1)S(1)} fusion(bf16[16,256,2,128]{3,2,1,0:T(2,128)(2,1)} %reshape.79, f32[16,2,64]{2,1,0:T(2,128)S(1)} %get-tuple-element.6, f32[16,2,256,64]{2,3,1,0:T(8,128)} %copy-done.3), kind=kOutput, calls=%fused_computation.34 | convolution fusion | flops 137103616 | bytes 4726784 | tf_op jit(solution)/shard_map/chqk,ckhd->cqhd/dot_general | solution.py:50
  432.1 66.1 %reduce-scatter.5.cloned.1.call-done = bf16[512,512]{1,0:T(8,128)(2,1)} async-done(((bf16[8192,512]{1,0:T(8,128)(2,1)}), bf16[512,512]{1,0:T(8,128)(2,1)}) %reduce-scatter.5.cloned.1.call-update) | async-done | bytes 524304 | tf_op jit(solution)/shard_map/reduce_scatter | solution.py:91
  (59 shorter events, 23.7 us)
Async XLA Ops:
  7.2 173.5 %all-gather.5.cloned.1.call-start = ((), (), s32[]{:S(2)}) async-start(), calls=%async_computation.4 | async-start | bytes 2228224 | tf_op jit(solution)/shard_map/all_gather | solution.py:35
  8.7 2.0 copy-start.4
  132.3 5.8 %copy-start.7 = (s32[16,2]{0,1:T(2,128)S(1)}, s32[16,2]{0,1:T(2,128)}, u32[]{:S(2)}) copy-start(s32[16,2]{0,1:T(2,128)} %param.10) | copy-start | bytes 388
  132.3 6.2 %copy-start.5 = (bf16[1024,256]{1,0:T(8,128)(2,1)S(1)}, bf16[1024,256]{1,0:T(8,128)(2,1)}, u32[]{:S(2)}) copy-start(bf16[1024,256]{1,0:T(8,128)(2,1)} %param.6) | copy-start | bytes 1572868
  132.3 6.3 %copy-start.6 = (bf16[1024,256]{1,0:T(8,128)(2,1)S(1)}, bf16[1024,256]{1,0:T(8,128)(2,1)}, u32[]{:S(2)}) copy-start(bf16[1024,256]{1,0:T(8,128)(2,1)} %param.11) | copy-start | bytes 1572868
  132.3 100.7 %all-gather.3.cloned.1.call-start = ((), (), s32[]{:S(2)}) async-start(), calls=%async_computation.3 | async-start | bytes 2228224 | tf_op jit(solution)/shard_map/all_gather | solution.py:36
  137.9 263.0 %reduce-scatter.3.cloned.1.call-start = ((), (), s32[]{:S(2)}) async-start(), calls=%async_computation.5 | async-start | bytes 4456448 | tf_op jit(solution)/shard_map/reduce_scatter | solution.py:85
  240.6 2.8 copy-start.2
  241.5 4.2 copy-start.3
  303.4 4.8 copy-start
  303.4 5.9 %copy-start.1 = (f32[32,128,256]{2,0,1:T(8,128)S(1)}, f32[32,128,256]{2,0,1:T(8,128)}, u32[]{:S(2)}) copy-start(f32[32,128,256]{2,0,1:T(8,128)} %copy.106) | copy-start | bytes 12582916
  318.6 179.6 %reduce-scatter.5.cloned.1.call-start = ((), (), s32[]{:S(2)}) async-start(), calls=%async_computation.6 | async-start | bytes 8912896 | tf_op jit(solution)/shard_map/reduce_scatter | solution.py:91
Sparse Core Ops, SparseCore 0:
  132.4 48.1 all-gather.4
  183.6 49.3 all-gather.2
  318.7 82.0 reduce-scatter.2
  408.8 89.4 reduce-scatter.4
